TPU v7x, 512 devices: a whole 4x8x8 slice. The times are simulated.
512 devices in a mesh: seq: 128 (over z, y, core), tp: 4 (over x).
Axes of the slice: x: 4, y: 8, z: 8, core: 2. Of those that a mesh axis runs over, the one named last changes fastest.
Arguments:
- queries: bfloat16 [4096, 1536], P('seq', 'tp'), may hold values from -100 to 100
- new_keys: bfloat16 [4096, 1536], P('seq', 'tp'), may hold values from -16 to 16
- new_values: bfloat16 [4096, 1536], P('seq', 'tp'), may hold values from -6 to 6
- forget_logit: float32 [24, 4096], P('tp', 'seq'), may hold values from 0 to 20
- cache_keys: bfloat16 [262144, 1536], P('seq', 'tp'), may hold values from -16 to 16
- cache_values: bfloat16 [262144, 1536], P('seq', 'tp'), may hold values from -6 to 6
- cache_decay: float32 [24, 262144], P('tp', 'seq'), may hold values from 0 to 32768, as said below
- slot_page: int32 [2048], P('seq'), may hold values from 0 to 255, as said below
- cache_len: int32 [8], replicated, may hold values from 1 to 32768, as said below
- residual: bfloat16 [4096, 1536], P('seq', 'tp'), may hold values from -6 to 6
- out_weight: bfloat16 [1536, 1536], P('tp'), may hold values from -0.15625 to 0.15625
Outputs:
- layer_out: bfloat16 [4096, 1536], P('seq', 'tp')
- new_forget: float32 [24, 4096], P('tp', 'seq')
Inputs may be any that keep to these rules, and one draw needn't show every extreme that they name: `slot_page`: within the slots of each request, every page number 0 to 255 stands exactly once. `cache_len`: some request has exactly 32768 cached tokens. `cache_decay`: over the live slots of one request and one head it does not rise as the position rises.
All inputs are finite; a program needn't handle non-finite values.
Results may differ from a plain program's by a relative error of at most 0.0075.
Values may be sent and summed in bfloat16 or wider, within the bound.
A program may use at most 64 MiB of HBM per device.

v0:
```python
import jax
import jax.numpy as jnp
from jax import lax
from jax.sharding import PartitionSpec as P

HEAD_DIM = 64
REQUEST_TOTAL = 8
PAGE = 128


MASKED_SCORE = -1e30


def entering(value, axis, join, neutral):
    count, mine = (lax.axis_size(axis), lax.axis_index(axis))
    pieces = jax.tree.map(lambda part: lax.all_gather(part, axis), value)
    total = jax.tree.map(
        lambda part, zero: jnp.full_like(part, 0) + jnp.asarray(zero, part.dtype), value, neutral
    )

    def hop(position, total):
        longer = join(total, jax.tree.map(lambda part: part[position], pieces))
        return jax.tree.map(lambda new, old: jnp.where(position < mine, new, old), longer, total)

    return lax.fori_loop(0, count - 1, hop, total)


def from_partner(x, axis, apart):
    return lax.ppermute(x, axis, [(i, i ^ 1 << apart) for i in range(lax.axis_size(axis))])


def merge_parts(left_part, right_part):
    highest = jnp.maximum(left_part[0], right_part[0])
    scale_left = jnp.exp(left_part[0] - highest)
    scale_right = jnp.exp(right_part[0] - highest)
    row_count, head_count = highest.shape
    weighted = (
        left_part[2].reshape(row_count, head_count, -1) * scale_left[:, :, None]
        + right_part[2].reshape(row_count, head_count, -1) * scale_right[:, :, None]
    )
    return (
        highest,
        left_part[1] * scale_left + right_part[1] * scale_right,
        weighted.reshape(row_count, -1),
    )


def affine_pair(before_part, after_part):
    return (before_part[0] * after_part[0], after_part[0] * before_part[1] + after_part[1])


def attend(carry, query_heads, key_rows, value_rows, key_decay, key_alive, query_forget):
    running_max, running_total, running_sum = carry
    scores = jnp.einsum(
        "ihd,khd->ihk", query_heads, key_rows, preferred_element_type=jnp.float32
    ) * HEAD_DIM ** (-0.5)
    scores = scores + query_forget[:, :, None] - key_decay[None, :, :]
    key_mask = key_alive[:, None, :]
    scores = jnp.where(key_mask, scores, MASKED_SCORE)
    highest = jnp.maximum(running_max, jnp.max(scores, axis=2))
    weights = jnp.where(key_mask, jnp.exp(scores - highest[:, :, None]), 0.0)
    factor = jnp.exp(running_max - highest)
    denominator = running_total * factor + jnp.sum(weights, axis=2)
    weighted = running_sum * factor[:, :, None] + jnp.einsum(
        "ihk,khd->ihd", weights.astype(jnp.bfloat16), value_rows, preferred_element_type=jnp.float32
    )
    return (highest, denominator, weighted)


def shards(
    queries,
    new_keys,
    new_values,
    forget_logit,
    cache_keys,
    cache_values,
    cache_decay,
    slot_page,
    cache_len,
    residual,
    out_weight,
):
    own_rows, feature_width = queries.shape
    head_count = forget_logit.shape[0]
    head_depth = feature_width // head_count
    group_size = lax.axis_size("seq") // REQUEST_TOTAL
    levels = group_size.bit_length() - 1
    position = lax.axis_index("seq")
    block_index = position % group_size
    request = position // group_size
    group_rows = own_rows * group_size
    log_forget = jax.nn.log_sigmoid(forget_logit)
    running = jnp.cumsum(log_forget, axis=1)
    keep_flag = jnp.where(block_index == group_size - 1, 0.0, 1.0) * jnp.ones(
        (head_count,), jnp.float32
    )
    carried = entering(
        (keep_flag, keep_flag * running[:, -1]),
        "seq",
        affine_pair,
        (jnp.ones((head_count,), jnp.float32), jnp.zeros((head_count,), jnp.float32)),
    )
    own_forget = running + carried[1][:, None]
    group_queries = queries
    group_forget = own_forget
    for which_bit in range(levels):
        other_queries, other_forget = (
            from_partner(group_queries, "seq", which_bit),
            from_partner(group_forget.astype(jnp.bfloat16), "seq", which_bit).astype(
                group_forget.dtype
            ),
        )
        upper_half = block_index // (1 << which_bit) % 2 == 1
        group_queries = jnp.where(
            upper_half,
            jnp.concatenate([other_queries, group_queries], 0),
            jnp.concatenate([group_queries, other_queries], 0),
        )
        group_forget = jnp.where(
            upper_half,
            jnp.concatenate([other_forget, group_forget], 1),
            jnp.concatenate([group_forget, other_forget], 1),
        )
    query_heads = group_queries.reshape(group_rows, head_count, head_depth)
    query_forget = group_forget.T
    slot_count = cache_keys.shape[0]
    key_span = 512
    span_count = slot_count // key_span
    token_positions = (
        slot_page[:, None] * PAGE + jnp.arange(PAGE, dtype=jnp.int32)[None, :]
    ).reshape(slot_count)
    request_length = jnp.sum(
        jnp.where(jnp.arange(REQUEST_TOTAL, dtype=jnp.int32) == request, cache_len, 0)
    )
    alive_slots = (token_positions < request_length).reshape(span_count, 1, key_span)
    key_blocks = cache_keys.reshape(span_count, key_span, head_count, head_depth)
    value_blocks = cache_values.reshape(span_count, key_span, head_count, head_depth)
    decay_blocks = cache_decay.reshape(head_count, span_count, key_span).transpose(1, 0, 2)
    initial = (
        jnp.full((group_rows, head_count), MASKED_SCORE, jnp.float32),
        jnp.zeros((group_rows, head_count), jnp.float32),
        jnp.zeros((group_rows, head_count, head_depth), jnp.float32),
    )

    def scan_step(carry, segment):
        key_rows, value_rows, key_decay, key_alive = segment
        return (
            attend(carry, query_heads, key_rows, value_rows, key_decay, key_alive, query_forget),
            None,
        )

    running_state, _ = lax.scan(
        scan_step, initial, (key_blocks, value_blocks, decay_blocks, alive_slots)
    )
    query_index = jnp.arange(group_rows, dtype=jnp.int32)
    fresh_index = block_index * own_rows + jnp.arange(own_rows, dtype=jnp.int32)
    causal = fresh_index[None, :] <= query_index[:, None]
    running_state = attend(
        running_state,
        query_heads,
        new_keys.reshape(own_rows, head_count, head_depth),
        new_values.reshape(own_rows, head_count, head_depth),
        own_forget,
        causal,
        query_forget,
    )
    partials = (
        running_state[0],
        running_state[1],
        running_state[2].reshape(group_rows, feature_width),
    )
    for which_bit in range(levels):
        partner = from_partner((partials[0], partials[1], partials[2]), "seq", which_bit)
        partials = merge_parts(partials, partner)
    partials = tuple(
        (
            lax.dynamic_slice_in_dim(member, block_index * own_rows, own_rows, 0)
            for member in partials
        )
    )
    denominator = partials[1]
    attention = (
        (partials[2].reshape(own_rows, head_count, head_depth) / denominator[:, :, None])
        .reshape(own_rows, feature_width)
        .astype(jnp.bfloat16)
    )
    projected = jnp.dot(attention, out_weight, preferred_element_type=jnp.float32)
    summed = lax.psum_scatter(
        projected.astype(jnp.bfloat16), "tp", scatter_dimension=1, tiled=True
    ).astype(jnp.float32)
    layer_out = (residual.astype(jnp.float32) + summed).astype(jnp.bfloat16)
    return (layer_out, own_forget)


def solution(mesh):
    return jax.shard_map(
        shards,
        mesh=mesh,
        in_specs=(
            P("seq", "tp"),
            P("seq", "tp"),
            P("seq", "tp"),
            P("tp", "seq"),
            P("seq", "tp"),
            P("seq", "tp"),
            P("tp", "seq"),
            P("seq"),
            P(),
            P("seq", "tp"),
            P("tp", None),
        ),
        out_specs=(P("seq", "tp"), P("tp", "seq")),
        check_vma=False,
    )
```

profile of v0, /device:TPU:1, one launch (start us, length us, event | category | flops | bytes accessed | tf_op | source)
XLA Modules:
  0.0 550.4 jit_solution(14507919656484522444)
XLA Ops:
  7.2 8.9 %collective-permute-start = (bf16[32,384]{1,0:T(8,128)(2,1)}, bf16[32,384]{1,0:T(8,128)(2,1)}, u32[]{:S(2)}, u32[]{:S(2)}) collective-permute-start(bf16[32,384]{1,0:T(8,128)(2,1)} %param.15), channel_id=1, source_target_pairs={{0,4},{4,0},{8,12},{12,8},{16,20},{20,16},{24,28},{28,24},{32,36},... | collective-permute-start | bytes 73736 | tf_op jit(solution)/shard_map/ppermute | solution.py:29
  19.9 251.9 %all-reduce.2 = (f32[128]{0:T(128)S(1)}, f32[768]{0:T(1024)S(1)}) all-reduce(f32[128]{0:T(128)S(1)} %dynamic-update-slice, f32[768]{0:T(1024)S(1)} %dynamic-update-slice.1), channel_id=2, replica_groups=mesh['seq'=128,'tp'=4] {'seq'}, use_global_device_ids=true, to_apply=%add | all-reduce | flops 896 | bytes 7168
  272.0 5.3 while.29
  277.3 7.6 %collective-permute-start.4 = (bf16[6,32]{1,0:T(8,128)(2,1)S(1)}, bf16[6,32]{1,0:T(8,128)(2,1)S(1)}, u32[]{:S(2)}, u32[]{:S(2)}) collective-permute-start(bf16[6,32]{1,0:T(8,128)(2,1)S(1)} %get-tuple-element.279), channel_id=1, source_target_pairs={{0,4},{4,0},{8,12},{12,8},{16,20},{20,16},{24,28},{28,24},{32,36},... | collective-permute-start | bytes 1160 | tf_op jit(solution)/shard_map/ppermute | solution.py:29
  288.4 1.9 collective-permute-start.5
  290.4 2.4 collective-permute-done.5
  292.8 1.9 collective-permute-start.6
  294.8 3.3 collective-permute-done.6
  298.7 1.9 collective-permute-start.7
  302.7 2.6 copy.34
  305.4 2.9 reshape.177
  309.7 2.6 copy.40
  312.4 2.9 reshape.179
  315.3 1.6 copy.42
  320.1 1.9 collective-permute-start.1
  325.0 1.9 collective-permute-start.2
  328.1 4.1 collective-permute-done.2
  332.2 7.3 %collective-permute-start.3 = (bf16[256,384]{1,0:T(8,128)(2,1)S(1)}, bf16[256,384]{1,0:T(8,128)(2,1)S(1)}, u32[]{:S(2)}, u32[]{:S(2)}) collective-permute-start(bf16[256,384]{1,0:T(8,128)(2,1)S(1)} %maximum_select_fusion.1), channel_id=1, source_target_pairs={{0,32},{4,36},{8,40},{12,44},{16,48},{20,52},{24,56},{28,60},{32,0... | collective-permute-start | bytes 589832 | tf_op jit(solution)/shard_map/ppermute | solution.py:29
  339.8 2.7 collective-permute-done.3
  342.8 57.5 %while.30 = (s32[]{:T(128)}, f32[512,6]{0,1:T(8,128)S(1)}, f32[512,6]{0,1:T(8,128)}, f32[512,6,64]{0,2,1:T(8,128)S(1)}, pred[4,1,512]{2,1,0:T(4,128)(4,1)}, /*in...) while((s32[]{:T(128)}, f32[512,6]{0,1:T(8,128)S(1)}, ...), condition=%wide.region_7.8_spmd.clone, body=%wide.region_4.7_spmd.clone.sunk | while | flops 433142784 | bytes 47188716 | solution.py:152
  344.3 5.2 fusion.65
  349.5 4.2 fusion.66
  354.1 3.1 fusion.68
  358.6 5.2 fusion.65
  363.9 4.2 fusion.66
  368.5 3.1 fusion.68
  373.0 5.2 fusion.65
  378.2 4.2 fusion.66
  382.9 3.1 fusion.68
  387.4 5.2 fusion.65
  392.6 4.2 fusion.66
  397.3 3.1 fusion.68
  401.8 9.3 %collective-permute-start.9 = (f32[512,384]{0,1:T(8,128)S(1)}, f32[512,384]{0,1:T(8,128)S(1)}, u32[]{:S(2)}, u32[]{:S(2)}) collective-permute-start(f32[512,384]{0,1:T(8,128)S(1)} %bitcast.111), channel_id=1, source_target_pairs={{0,4},{4,0},{8,12},{12,8},{16,20},{20,16},{24,28},{28,24},{32,36},... | collective-permute-start | bytes 2359304 | tf_op jit(solution)/shard_map/ppermute | solution.py:29
  411.1 1.9 collective-permute-start.16
  413.0 2.4 collective-permute-start.8
  416.5 1.9 collective-permute-start.11
  418.4 3.4 collective-permute-start.17
  421.8 1.9 collective-permute-start.10
  423.7 13.8 %collective-permute-done.17 = f32[512,6]{0,1:T(8,128)S(1)} collective-permute-done((f32[512,6]{0,1:T(8,128)S(1)}, f32[512,6]{0,1:T(8,128)S(1)}, u32[]{:S(2)}, u32[]{:S(2)}) %collective-permute-start.17) | collective-permute-done | bytes 12320 | tf_op jit(solution)/shard_map/ppermute | solution.py:29
  438.1 1.9 collective-permute-start.13
  440.0 4.3 collective-permute-start.18
  444.3 1.9 collective-permute-start.12
  446.2 31.9 %collective-permute-done.18 = f32[512,6]{0,1:T(8,128)S(1)} collective-permute-done((f32[512,6]{0,1:T(8,128)S(1)}, f32[512,6]{0,1:T(8,128)S(1)}, u32[]{:S(2)}, u32[]{:S(2)}) %collective-permute-start.18) | collective-permute-done | bytes 12320 | tf_op jit(solution)/shard_map/ppermute | solution.py:29
  478.7 7.7 %collective-permute-start.15 = (f32[512,384]{0,1:T(8,128)S(1)}, f32[512,384]{0,1:T(8,128)S(1)}, u32[]{:S(2)}, u32[]{:S(2)}) collective-permute-start(f32[512,384]{0,1:T(8,128)S(1)} %bitcast.110), channel_id=1, source_target_pairs={{0,32},{4,36},{8,40},{12,44},{16,48},{20,52},{24,56},{28,60},{32,0... | collective-permute-start | bytes 2359304 | tf_op jit(solution)/shard_map/ppermute | solution.py:29
  486.4 1.9 collective-permute-start.14
  488.4 7.3 %collective-permute-start.19 = (f32[512,6]{0,1:T(8,128)S(1)}, f32[512,6]{0,1:T(8,128)S(1)}, u32[]{:S(2)}, u32[]{:S(2)}) collective-permute-start(f32[512,6]{0,1:T(8,128)S(1)} %get-tuple-element.259), channel_id=1, source_target_pairs={{0,32},{4,36},{8,40},{12,44},{16,48},{20,52},{24,56},{28,60},{32,0... | collective-permute-start | bytes 36872 | tf_op jit(solution)/shard_map/ppermute | solution.py:29
  495.6 26.3 %collective-permute-done.14 = f32[512,6]{0,1:T(8,128)S(1)} collective-permute-done((f32[512,6]{0,1:T(8,128)S(1)}, f32[512,6]{0,1:T(8,128)S(1)}, u32[]{:S(2)}, u32[]{:S(2)}) %collective-permute-start.14) | collective-permute-done | bytes 12320 | tf_op jit(solution)/shard_map/ppermute | solution.py:29
  524.1 17.9 %reduce-scatter.4.cloned.1.call-done = bf16[384,32]{1,0:T(8,128)(2,1)} async-done(((bf16[1536,32]{1,0:T(8,128)(2,1)}), bf16[384,32]{1,0:T(8,128)(2,1)}) %reduce-scatter.4.cloned.1.call-update) | async-done | bytes 24592
  (261 shorter events, 36.0 us)
Async XLA Ops:
  7.2 515.6 %copy-start = (bf16[384,1536]{1,0:T(8,128)(2,1)S(1)}, bf16[384,1536]{1,0:T(8,128)(2,1)}, u32[]{:S(2)}) copy-start(bf16[384,1536]{1,0:T(8,128)(2,1)} %param.25) | copy-start | bytes 3538948
  7.2 534.8 %reduce-scatter.4.cloned.1.call-start = ((), (), s32[]{:S(2)}) async-start(), calls=%async_computation.1 | async-start | bytes 491520
  7.2 312.0 %collective-permute-start = (bf16[32,384]{1,0:T(8,128)(2,1)}, bf16[32,384]{1,0:T(8,128)(2,1)}, u32[]{:S(2)}, u32[]{:S(2)}) collective-permute-start(bf16[32,384]{1,0:T(8,128)(2,1)} %param.15), channel_id=1, source_target_pairs={{0,4},{4,0},{8,12},{12,8},{16,20},{20,16},{24,28},{28,24},{32,36},... | collective-permute-start | bytes 73736 | tf_op jit(solution)/shard_map/ppermute | solution.py:29
  277.3 23.9 %copy-start.5 = (f32[6,32]{1,0:T(8,128)}, f32[6,32]{1,0:T(8,128)S(1)}, u32[]{:S(2)}) copy-start(f32[6,32]{1,0:T(8,128)S(1)} %get-tuple-element.280) | copy-start | bytes 2308
  277.3 11.0 %collective-permute-start.4 = (bf16[6,32]{1,0:T(8,128)(2,1)S(1)}, bf16[6,32]{1,0:T(8,128)(2,1)S(1)}, u32[]{:S(2)}, u32[]{:S(2)}) collective-permute-start(bf16[6,32]{1,0:T(8,128)(2,1)S(1)} %get-tuple-element.279), channel_id=1, source_target_pairs={{0,4},{4,0},{8,12},{12,8},{16,20},{20,16},{24,28},{28,24},{32,36},... | collective-permute-start | bytes 1160 | tf_op jit(solution)/shard_map/ppermute | solution.py:29
  288.4 4.3 collective-permute-start.5
  292.8 5.2 collective-permute-start.6
  298.7 19.9 %collective-permute-start.7 = (bf16[6,256]{1,0:T(8,128)(2,1)}, bf16[6,256]{1,0:T(8,128)(2,1)}, u32[]{:S(2)}, u32[]{:S(2)}) collective-permute-start(bf16[6,256]{1,0:T(8,128)(2,1)} %get-tuple-element.273), channel_id=1, source_target_pairs={{0,32},{4,36},{8,40},{12,44},{16,48},{20,52},{24,56},{28,60},{32,0... | collective-permute-start | bytes 9224 | tf_op jit(solution)/shard_map/ppermute | solution.py:29
  320.1 4.8 collective-permute-start.1
  325.0 7.2 %collective-permute-start.2 = (bf16[128,384]{1,0:T(8,128)(2,1)S(1)}, bf16[128,384]{1,0:T(8,128)(2,1)S(1)}, u32[]{:S(2)}, u32[]{:S(2)}) collective-permute-start(bf16[128,384]{1,0:T(8,128)(2,1)S(1)} %maximum_select_fusion.3), channel_id=1, source_target_pairs={{0,16},{4,20},{8,24},{12,28},{16,0},{20,4},{24,8},{28,12},{32,48},... | collective-permute-start | bytes 294920 | tf_op jit(solution)/shard_map/ppermute | solution.py:29
  332.2 10.3 %collective-permute-start.3 = (bf16[256,384]{1,0:T(8,128)(2,1)S(1)}, bf16[256,384]{1,0:T(8,128)(2,1)S(1)}, u32[]{:S(2)}, u32[]{:S(2)}) collective-permute-start(bf16[256,384]{1,0:T(8,128)(2,1)S(1)} %maximum_select_fusion.1), channel_id=1, source_target_pairs={{0,32},{4,36},{8,40},{12,44},{16,48},{20,52},{24,56},{28,60},{32,0... | collective-permute-start | bytes 589832 | tf_op jit(solution)/shard_map/ppermute | solution.py:29
  342.8 57.5 %copy-start.4 = (pred[512,32]{0,1:T(8,128)(4,1)S(1)}, pred[512,32]{0,1:T(8,128)(4,1)}, u32[]{:S(2)}) copy-start(pred[512,32]{0,1:T(8,128)(4,1)} %iota_compare_fusion) | copy-start | bytes 49156
  342.8 57.5 %copy-start.6 = (f32[6,32]{1,0:T(8,128)S(1)}, f32[6,32]{1,0:T(8,128)}, u32[]{:S(2)}) copy-start(f32[6,32]{1,0:T(8,128)} %copy-done.5) | copy-start | bytes 2308
  344.2 9.5 %copy-start.2 = (f32[512,6]{0,1:T(8,128)S(1)}, f32[512,6]{0,1:T(8,128)}, u32[]{:S(2)}) copy-start(f32[512,6]{0,1:T(8,128)} %get-tuple-element.422) | copy-start | bytes 36868 | tf_op jit(solution)/shard_map/while
  349.5 4.6 copy-start.1
  353.8 3.4 copy-start.3
  358.6 9.5 %copy-start.2 = (f32[512,6]{0,1:T(8,128)S(1)}, f32[512,6]{0,1:T(8,128)}, u32[]{:S(2)}) copy-start(f32[512,6]{0,1:T(8,128)} %get-tuple-element.422) | copy-start | bytes 36868 | tf_op jit(solution)/shard_map/while
  363.9 4.6 copy-start.1
  368.1 3.4 copy-start.3
  373.0 9.5 %copy-start.2 = (f32[512,6]{0,1:T(8,128)S(1)}, f32[512,6]{0,1:T(8,128)}, u32[]{:S(2)}) copy-start(f32[512,6]{0,1:T(8,128)} %get-tuple-element.422) | copy-start | bytes 36868 | tf_op jit(solution)/shard_map/while
  378.2 4.6 copy-start.1
  382.5 3.4 copy-start.3
  387.4 9.5 %copy-start.2 = (f32[512,6]{0,1:T(8,128)S(1)}, f32[512,6]{0,1:T(8,128)}, u32[]{:S(2)}) copy-start(f32[512,6]{0,1:T(8,128)} %get-tuple-element.422) | copy-start | bytes 36868 | tf_op jit(solution)/shard_map/while
  392.6 4.6 copy-start.1
  396.9 3.4 copy-start.3
  401.8 14.5 %collective-permute-start.9 = (f32[512,384]{0,1:T(8,128)S(1)}, f32[512,384]{0,1:T(8,128)S(1)}, u32[]{:S(2)}, u32[]{:S(2)}) collective-permute-start(f32[512,384]{0,1:T(8,128)S(1)} %bitcast.111), channel_id=1, source_target_pairs={{0,4},{4,0},{8,12},{12,8},{16,20},{20,16},{24,28},{28,24},{32,36},... | collective-permute-start | bytes 2359304 | tf_op jit(solution)/shard_map/ppermute | solution.py:29
  411.1 4.3 collective-permute-start.16
  413.0 3.2 collective-permute-start.8
  416.3 126.6 %copy-start.7 = (bf16[32,384]{1,0:T(8,128)(2,1)S(1)}, bf16[32,384]{1,0:T(8,128)(2,1)}, u32[]{:S(2)}) copy-start(bf16[32,384]{1,0:T(8,128)(2,1)} %param.24) | copy-start | bytes 73732
  416.5 21.4 %collective-permute-start.11 = (f32[512,384]{0,1:T(8,128)S(1)}, f32[512,384]{0,1:T(8,128)S(1)}, u32[]{:S(2)}, u32[]{:S(2)}) collective-permute-start(f32[512,384]{0,1:T(8,128)S(1)} %bitcast.112), channel_id=1, source_target_pairs={{0,8},{4,12},{8,0},{12,4},{16,24},{20,28},{24,16},{28,20},{32,40},... | collective-permute-start | bytes 2359304 | tf_op jit(solution)/shard_map/ppermute | solution.py:29
  418.4 19.1 %collective-permute-start.17 = (f32[512,6]{0,1:T(8,128)S(1)}, f32[512,6]{0,1:T(8,128)S(1)}, u32[]{:S(2)}, u32[]{:S(2)}) collective-permute-start(f32[512,6]{0,1:T(8,128)S(1)} %get-tuple-element.267), channel_id=1, source_target_pairs={{0,8},{4,12},{8,0},{12,4},{16,24},{20,28},{24,16},{28,20},{32,40},... | collective-permute-start | bytes 36872 | tf_op jit(solution)/shard_map/ppermute | solution.py:29
  421.8 16.1 %collective-permute-start.10 = (f32[512,6]{0,1:T(8,128)S(1)}, f32[512,6]{0,1:T(8,128)S(1)}, u32[]{:S(2)}, u32[]{:S(2)}) collective-permute-start(f32[512,6]{0,1:T(8,128)S(1)} %get-tuple-element.270), channel_id=1, source_target_pairs={{0,8},{4,12},{8,0},{12,4},{16,24},{20,28},{24,16},{28,20},{32,40},... | collective-permute-start | bytes 36872 | tf_op jit(solution)/shard_map/ppermute | solution.py:29
  438.1 40.4 %collective-permute-start.13 = (f32[512,384]{0,1:T(8,128)S(1)}, f32[512,384]{0,1:T(8,128)S(1)}, u32[]{:S(2)}, u32[]{:S(2)}) collective-permute-start(f32[512,384]{0,1:T(8,128)S(1)} %bitcast.113), channel_id=1, source_target_pairs={{0,16},{4,20},{8,24},{12,28},{16,0},{20,4},{24,8},{28,12},{32,48},... | collective-permute-start | bytes 2359304 | tf_op jit(solution)/shard_map/ppermute | solution.py:29
  440.0 38.1 %collective-permute-start.18 = (f32[512,6]{0,1:T(8,128)S(1)}, f32[512,6]{0,1:T(8,128)S(1)}, u32[]{:S(2)}, u32[]{:S(2)}) collective-permute-start(f32[512,6]{0,1:T(8,128)S(1)} %get-tuple-element.263), channel_id=1, source_target_pairs={{0,16},{4,20},{8,24},{12,28},{16,0},{20,4},{24,8},{28,12},{32,48},... | collective-permute-start | bytes 36872 | tf_op jit(solution)/shard_map/ppermute | solution.py:29
  444.3 34.1 %collective-permute-start.12 = (f32[512,6]{0,1:T(8,128)S(1)}, f32[512,6]{0,1:T(8,128)S(1)}, u32[]{:S(2)}, u32[]{:S(2)}) collective-permute-start(f32[512,6]{0,1:T(8,128)S(1)} %get-tuple-element.266), channel_id=1, source_target_pairs={{0,16},{4,20},{8,24},{12,28},{16,0},{20,4},{24,8},{28,12},{32,48},... | collective-permute-start | bytes 36872 | tf_op jit(solution)/shard_map/ppermute | solution.py:29
  478.7 43.7 %collective-permute-start.15 = (f32[512,384]{0,1:T(8,128)S(1)}, f32[512,384]{0,1:T(8,128)S(1)}, u32[]{:S(2)}, u32[]{:S(2)}) collective-permute-start(f32[512,384]{0,1:T(8,128)S(1)} %bitcast.110), channel_id=1, source_target_pairs={{0,32},{4,36},{8,40},{12,44},{16,48},{20,52},{24,56},{28,60},{32,0... | collective-permute-start | bytes 2359304 | tf_op jit(solution)/shard_map/ppermute | solution.py:29
  486.4 35.6 %collective-permute-start.14 = (f32[512,6]{0,1:T(8,128)S(1)}, f32[512,6]{0,1:T(8,128)S(1)}, u32[]{:S(2)}, u32[]{:S(2)}) collective-permute-start(f32[512,6]{0,1:T(8,128)S(1)} %get-tuple-element.262), channel_id=1, source_target_pairs={{0,32},{4,36},{8,40},{12,44},{16,48},{20,52},{24,56},{28,60},{32,0... | collective-permute-start | bytes 36872 | tf_op jit(solution)/shard_map/ppermute | solution.py:29
  488.4 34.0 %collective-permute-start.19 = (f32[512,6]{0,1:T(8,128)S(1)}, f32[512,6]{0,1:T(8,128)S(1)}, u32[]{:S(2)}, u32[]{:S(2)}) collective-permute-start(f32[512,6]{0,1:T(8,128)S(1)} %get-tuple-element.259), channel_id=1, source_target_pairs={{0,32},{4,36},{8,40},{12,44},{16,48},{20,52},{24,56},{28,60},{32,0... | collective-permute-start | bytes 36872 | tf_op jit(solution)/shard_map/ppermute | solution.py:29
Sparse Core Ops, SparseCore 0:
  524.2 17.6 reduce-scatter.3
where the time goes:
time: 554 us; the launch traced here: 550 us
  blocking collectives  252 us (45%)
  waiting for transfers between devices  105 us (19%)
  starting transfers between devices  79.2 us (14%)
  matrix products  34 us (6%)
  other arithmetic  31.6 us (6%)
  local copies, waits for them, and re-layouts  29.9 us (5%)
  between operations  15.2 us (3%)
    unnamed x1, blocking collectives  252 us
    ppermute x20, waiting for transfers between devices, from_partner(): lax.ppermute(x, axis, [(i, i ^ 1 << apart) for i in range(lax.axis_size(a...  87.5 us
    ppermute x20, starting transfers between devices, from_partner(): lax.ppermute(x, axis, [(i, i ^ 1 << apart) for i in range(lax.axis_size(a...  79.2 us
    dot_general x5, matrix products, attend(): jnp.einsum('ihd,khd->ihk', query_heads, key_rows, preferred_element_type=...  21.1 us
    unnamed x2, waiting for transfers between devices  17.9 us
    reduce_sum x5, other arithmetic, attend(): denominator = running_total * factor + jnp.sum(weights, axis=2)  17.1 us
    unnamed x23, local copies, waits for them, and re-layouts  13.9 us
    dot_general x5, matrix products, attend(): jnp.einsum('ihk,khd->ihd', weights.astype(jnp.bfloat16), value_rows, pref...  12.6 us
  transfers between devices with their start and end apart: 21, of which 13 were waited for; matrix products, arithmetic and copies ran while one was open for 6% of the time, Pallas kernels for 0%

commit v1 on v0

v1 whole, which is shorter than its diff:
```python
import functools

import jax
import jax.numpy as jnp
from jax import lax
from jax.experimental import pallas as pl
from jax.experimental.pallas import tpu as pltpu
from jax.sharding import PartitionSpec as P

HEAD_DIM = 64
PAGE = 128
CHIPS = 8
GROUP = 16
DEAD = 1e30
MESH = pl.DeviceIdType.MESH


def thirds(x):
    high = x.astype(jnp.bfloat16)
    rest = x - high.astype(jnp.float32)
    middle = rest.astype(jnp.bfloat16)
    low = (rest - middle.astype(jnp.float32)).astype(jnp.bfloat16)
    return high, middle, low


def layer_kernel(
    tp_count,
    q_ref,
    new_keys,
    new_values,
    logit_ref,
    cache_keys,
    cache_values,
    decay_ref,
    page_ref,
    length_ref,
    residual_ref,
    out_weight,
    out_ref,
    forget_ref,
    keys,
    values,
    weight,
    costs,
    queries,
    forget_tile,
    forget_all,
    parts_out,
    parts_in,
    shares_out,
    shares_in,
    local_sem,
    query_send,
    query_recv,
    forget_send,
    forget_recv,
    part_send,
    part_recv,
    share_send,
    share_recv,
):
    rows, width = q_ref.shape
    heads = width // HEAD_DIM
    pairs = heads // 2
    slots = cache_keys.shape[0]
    all_keys = keys.shape[0]
    seq = lax.axis_index("seq")
    tp = lax.axis_index("tp")
    request = seq // GROUP
    chip = (seq % GROUP) // 2
    core = seq % 2

    def device(chip_step, other):
        there = (chip + chip_step) % CHIPS
        return (request * GROUP + there * 2 + (1 - core if other else core), tp)

    local = [
        pltpu.make_async_copy(cache_keys, keys.at[pl.ds(0, slots)], local_sem.at[0]),
        pltpu.make_async_copy(new_keys, keys.at[pl.ds(slots, rows)], local_sem.at[1]),
        pltpu.make_async_copy(cache_values, values.at[pl.ds(0, slots)], local_sem.at[2]),
        pltpu.make_async_copy(new_values, values.at[pl.ds(slots, rows)], local_sem.at[3]),
        pltpu.make_async_copy(out_weight, weight, local_sem.at[4]),
        pltpu.make_async_copy(q_ref, queries.at[0, 0], local_sem.at[5]),
    ]
    for copy in local:
        copy.start()

    barrier = pltpu.get_barrier_semaphore()
    peers = [(step, other) for step in range(CHIPS) for other in (0, 1) if step or other]
    for step, other in peers:
        pl.semaphore_signal(barrier, inc=1, device_id=device(step, other), device_id_type=MESH)
    for step in range(1, tp_count):
        pl.semaphore_signal(
            barrier, inc=1, device_id=(seq, (tp + step) % tp_count), device_id_type=MESH
        )

    pad = all_keys - slots - rows
    keys[pl.ds(slots + rows, pad), :] = jnp.zeros((pad, width), keys.dtype)
    values[pl.ds(slots + rows, pad), :] = jnp.zeros((pad, width), values.dtype)
    forget_tile[...] = jnp.zeros(forget_tile.shape, jnp.float32)
    logit = logit_ref[...]
    forget_tile[pl.ds(0, heads), pl.ds(0, rows)] = -jnp.log1p(jnp.exp(-logit))
    lane = lax.broadcasted_iota(jnp.int32, forget_tile.shape, 1)
    running = forget_tile[...]
    reach = 1
    while reach < rows:
        running = running + jnp.where(lane >= reach, pltpu.roll(running, reach, 1), 0.0)
        reach *= 2
    total = jnp.sum(jnp.where(lane == rows - 1, running, 0.0), axis=1, keepdims=True)
    forget_tile[...] = jnp.broadcast_to(total, forget_tile.shape)
    pl.semaphore_wait(barrier, len(peers) + tp_count - 1)

    def query_direct(step):
        return pltpu.make_async_remote_copy(
            src_ref=q_ref,
            dst_ref=queries.at[(CHIPS - step) % CHIPS, 0 if step else 1],
            send_sem=query_send.at[step, 0],
            recv_sem=query_recv.at[(CHIPS - step) % CHIPS, 0 if step else 1],
            device_id=device(step, 0 if step else 1),
            device_id_type=MESH,
        )

    def query_relay(step):
        return pltpu.make_async_remote_copy(
            src_ref=queries.at[step, 0],
            dst_ref=queries.at[step, 1],
            send_sem=query_send.at[step, 1],
            recv_sem=query_recv.at[step, 1],
            device_id=device(0, 1),
            device_id_type=MESH,
        )

    def forget_copy(step, other):
        return pltpu.make_async_remote_copy(
            src_ref=forget_tile,
            dst_ref=forget_all.at[(CHIPS - step) % CHIPS, other],
            send_sem=forget_send.at[step, other],
            recv_sem=forget_recv.at[(CHIPS - step) % CHIPS, other],
            device_id=device(step, other),
            device_id_type=MESH,
        )

    near_first = [0, 1, 7, 2, 6, 3, 5, 4]
    for step in reversed(near_first):
        query_direct(step).start()
    for step, other in peers:
        forget_copy(step, other).start()

    length = length_ref[request]
    page_lane = lax.broadcasted_iota(jnp.int32, (1, PAGE), 1)
    for page in range(slots // PAGE):
        alive = page_ref[page] * PAGE + page_lane < length
        at = pl.ds(page * PAGE, PAGE)
        costs[pl.ds(0, heads), at] = jnp.where(alive, decay_ref[:, at], DEAD)

    for step, other in peers:
        forget_copy((CHIPS - step) % CHIPS, other).wait_recv()
    own_forget = running
    for step, other in peers:
        earlier = (core == 1) if step == 0 else (chip + step >= CHIPS)
        own_forget = own_forget + jnp.where(earlier, forget_all[step, other], 0.0)
    forget_ref[...] = own_forget[:heads, :rows]
    costs[:, pl.ds(slots, PAGE)] = jnp.where(lane < rows, own_forget, DEAD)

    for step in near_first[1:]:
        query_direct((CHIPS - step) % CHIPS).wait_recv()
        query_relay(step).start()
    for copy in local:
        copy.wait()
    query_direct(0).wait_recv()

    span = 2
    chunk = span * 2 * rows
    left = lax.broadcasted_iota(jnp.int32, (chunk, 2 * HEAD_DIM), 1) < HEAD_DIM
    key_lane = lax.broadcasted_iota(jnp.int32, (chunk, PAGE), 1)
    row_index = lax.broadcasted_iota(jnp.int32, (chunk, PAGE), 0)

    def part_copy(step, other):
        return pltpu.make_async_remote_copy(
            src_ref=parts_out.at[step, other],
            dst_ref=parts_in.at[(CHIPS - step) % CHIPS, other],
            send_sem=part_send.at[step, other],
            recv_sem=part_recv.at[(CHIPS - step) % CHIPS, other],
            device_id=device(step, other),
            device_id_type=MESH,
        )

    def step_of(turn):
        return ((turn + 1) // 2 * (2 * (turn % 2) - 1) + CHIPS) % CHIPS

    def attend(index):
        steps = [step_of(index * span + i) for i in range(span)]
        fresh = None
        for i, step in enumerate(steps):
            for other in (0, 1):
                first = (2 * i + other) * rows
                offset = row_index - first
                inside = (offset >= 0) & (offset < rows)
                later = jnp.where(
                    step == 0, jnp.where(core + other == 1, 1 - core, 0), (chip + step < CHIPS) * 1
                )
                own = jnp.where(step == 0, 1 - other, 0)
                limit = jnp.where(own == 1, offset, jnp.where(later == 1, rows, -1))
                fresh = jnp.where(inside, limit, 0 if fresh is None else fresh)
        visible = key_lane <= fresh
        pieces = [
            queries[step, other] for step in steps for other in (0, 1)
        ]
        stats = []
        outs = []
        for pair in range(pairs):
            at = slice(pair * 2 * HEAD_DIM, (pair + 1) * 2 * HEAD_DIM)
            q = jnp.concatenate([piece[:, at] for piece in pieces], axis=0)
            q = q * jnp.asarray(HEAD_DIM**-0.5, q.dtype)
            zero = jnp.zeros_like(q)
            value_pair = jnp.concatenate(
                [values[:, at], jnp.ones((all_keys, 2 * HEAD_DIM), values.dtype)], axis=1
            )
            both = []
            for side in (0, 1):
                head = pair * 2 + side
                q_side = jnp.where(left, q, zero) if side == 0 else jnp.where(left, zero, q)
                scores = lax.dot_general(
                    q_side,
                    keys[:, at],
                    (((1,), (1,)), ((), ())),
                    preferred_element_type=jnp.float32,
                )
                scores = scores - costs[pl.ds(head, 1), :]
                old = scores[:, :slots]
                new = jnp.where(visible, scores[:, slots:], -DEAD)
                highest = jnp.maximum(
                    jnp.max(old, axis=1, keepdims=True), jnp.max(new, axis=1, keepdims=True)
                )
                weights = jnp.concatenate(
                    [
                        jnp.exp(old - highest).astype(jnp.bfloat16),
                        jnp.exp(new - highest).astype(jnp.bfloat16),
                    ],
                    axis=1,
                )
                summed = jnp.dot(weights, value_pair, preferred_element_type=jnp.float32)
                sums = summed[:, 2 * HEAD_DIM :]
                both.append(summed[:, : 2 * HEAD_DIM] / sums)
                stats.append(highest + jnp.log(sums))
            outs.append(jnp.where(left, both[0], both[1]).astype(jnp.bfloat16))
        stat_lane = lax.broadcasted_iota(jnp.int32, (chunk, PAGE), 1)
        packed = jnp.zeros((chunk, PAGE), jnp.float32)
        for head, stat in enumerate(stats):
            high, middle, low = (t.astype(jnp.float32) for t in thirds(stat))
            packed = jnp.where(stat_lane == head, high, packed)
            packed = jnp.where(stat_lane == head + 8, middle, packed)
            packed = jnp.where(stat_lane == head + 16, low, packed)
        outs.append(packed.astype(jnp.bfloat16))
        for i, step in enumerate(steps):
            for other in (0, 1):
                first = (2 * i + other) * rows
                for j, out in enumerate(outs):
                    parts_out[step, other, :, pl.ds(j * 2 * HEAD_DIM, 2 * HEAD_DIM)] = out[
                        first : first + rows
                    ]
        return steps

    def wait_queries(step):
        pltpu.make_async_remote_copy(
            src_ref=queries.at[step, 0],
            dst_ref=queries.at[step, 1],
            send_sem=query_send.at[step, 1],
            recv_sem=query_recv.at[step, 1],
            device_id=device(0, 1),
            device_id_type=MESH,
        ).wait_recv()

    def turn(index, _):
        for i in range(span):
            step = step_of(index * span + i)

            @pl.when(step > 0)
            def _():
                wait_queries(step)

        steps = attend(index)
        for step in steps:

            @pl.when(step > 0)
            def _():
                part_copy(step, 0).start()

            part_copy(step, 1).start()
        return 0

    lax.fori_loop(0, CHIPS // span, turn, 0)

    stat_rows = []
    for step in range(CHIPS):
        for other in (0, 1):
            if step or other:
                part_copy((CHIPS - step) % CHIPS, other).wait_recv()
    def part(step, other, at):
        source = parts_in if (step or other) else parts_out
        return source[step, other, :, at]

    logs = []
    for step in range(CHIPS):
        for other in (0, 1):
            stat = part(step, other, pl.ds(width, PAGE)).astype(jnp.float32)
            logs.append(
                stat + pltpu.roll(stat, PAGE - 8, 1) + pltpu.roll(stat, PAGE - 16, 1)
            )
    top = functools.reduce(jnp.maximum, logs)
    shares = [jnp.exp(log - top) for log in logs]
    whole = functools.reduce(jnp.add, shares)
    stacked = jnp.concatenate([share / whole for share in shares], axis=0)
    stat_lane = lax.broadcasted_iota(jnp.int32, stacked.shape, 1)
    stacked = jnp.where(stat_lane < heads, stacked, 0.0)
    high, middle, _ = thirds(stacked)
    spread_row = lax.broadcasted_iota(jnp.int32, (2 * PAGE, width), 0) % PAGE
    spread_lane = lax.broadcasted_iota(jnp.int32, (2 * PAGE, width), 1) // HEAD_DIM
    spread = jnp.where(spread_row == spread_lane, 1.0, 0.0).astype(jnp.bfloat16)
    factors = jnp.dot(
        jnp.concatenate([high, middle], axis=1), spread, preferred_element_type=jnp.float32
    )
    attention = jnp.zeros((rows, width), jnp.float32)
    for step in range(CHIPS):
        for other in (0, 1):
            first = (2 * step + other) * rows
            attention = attention + factors[first : first + rows] * part(
                step, other, pl.ds(0, width)
            ).astype(jnp.float32)
    attention = attention.astype(jnp.bfloat16)

    def share_copy(step):
        return pltpu.make_async_remote_copy(
            src_ref=shares_out.at[step - 1],
            dst_ref=shares_in.at[tp_count - step - 1],
            send_sem=share_send.at[step - 1],
            recv_sem=share_recv.at[tp_count - step - 1],
            device_id=(seq, (tp + step) % tp_count),
            device_id_type=MESH,
        )

    def share(step):
        block = (tp + step) % tp_count
        columns = pl.ds(pl.multiple_of(block * width, PAGE), width)
        return jnp.dot(attention, weight[:, columns], preferred_element_type=jnp.float32)

    for step in range(1, tp_count):
        shares_out[step - 1] = share(step).astype(jnp.bfloat16)
        share_copy(step).start()
    summed = share(0)
    for step in range(1, tp_count):
        share_copy(step).wait_recv()
        summed = summed + shares_in[tp_count - step - 1].astype(jnp.float32)
    out_ref[...] = (residual_ref[...].astype(jnp.float32) + summed).astype(out_ref.dtype)

    for step in range(CHIPS):
        query_direct(step).wait_send()
        if step:
            query_relay(step).wait_send()
    for step, other in peers:
        forget_copy(step, other).wait_send()
        part_copy(step, other).wait_send()
    for step in range(1, tp_count):
        share_copy(step).wait_send()


def shards(
    queries,
    new_keys,
    new_values,
    forget_logit,
    cache_keys,
    cache_values,
    cache_decay,
    slot_page,
    cache_len,
    residual,
    out_weight,
):
    rows, width = queries.shape
    heads = forget_logit.shape[0]
    slots = cache_keys.shape[0]
    tp_count = lax.axis_size("tp")
    vmem = pl.BlockSpec(memory_space=pltpu.VMEM)
    smem = pl.BlockSpec(memory_space=pltpu.SMEM)
    anywhere = pl.BlockSpec(memory_space=pl.ANY)
    dma = pltpu.SemaphoreType.DMA
    half = jnp.bfloat16
    single = jnp.float32
    return pl.pallas_call(
        functools.partial(layer_kernel, tp_count),
        out_shape=(
            jax.ShapeDtypeStruct((rows, width), half),
            jax.ShapeDtypeStruct((heads, rows), single),
        ),
        in_specs=[
            vmem, anywhere, anywhere, vmem, anywhere, anywhere, vmem, smem, smem, vmem, anywhere,
        ],
        out_specs=(vmem, vmem),
        scratch_shapes=[
            pltpu.VMEM((slots + PAGE, width), half),
            pltpu.VMEM((slots + PAGE, width), half),
            pltpu.VMEM(out_weight.shape, half),
            pltpu.VMEM((8, slots + PAGE), single),
            pltpu.VMEM((CHIPS, 2, rows, width), half),
            pltpu.VMEM((8, PAGE), single),
            pltpu.VMEM((CHIPS, 2, 8, PAGE), single),
            pltpu.VMEM((CHIPS, 2, rows, width + PAGE), half),
            pltpu.VMEM((CHIPS, 2, rows, width + PAGE), half),
            pltpu.VMEM((max(tp_count - 1, 1), rows, width), half),
            pltpu.VMEM((max(tp_count - 1, 1), rows, width), half),
            dma((6,)),
            dma((CHIPS, 2)),
            dma((CHIPS, 2)),
            dma((CHIPS, 2)),
            dma((CHIPS, 2)),
            dma((CHIPS, 2)),
            dma((CHIPS, 2)),
            dma((max(tp_count - 1, 1),)),
            dma((max(tp_count - 1, 1),)),
        ],
        compiler_params=pltpu.CompilerParams(
            collective_id=0, has_side_effects=True, vmem_limit_bytes=60 * 1024 * 1024
        ),
        name="layer",
    )(
        queries, new_keys, new_values, forget_logit, cache_keys, cache_values, cache_decay,
        slot_page, cache_len, residual, out_weight,
    )


def solution(mesh):
    return jax.shard_map(
        shards,
        mesh=mesh,
        in_specs=(
            P("seq", "tp"),
            P("seq", "tp"),
            P("seq", "tp"),
            P("tp", "seq"),
            P("seq", "tp"),
            P("seq", "tp"),
            P("tp", "seq"),
            P("seq"),
            P(),
            P("seq", "tp"),
            P("tp", None),
        ),
        out_specs=(P("seq", "tp"), P("tp", "seq")),
        check_vma=False,
    )
```

time: 554 us -> 49.2 us (0.09)
  the two profiles are of different devices: /device:TPU:1 before, /device:TPU:136 now
where the time goes in v1:
time: 49.2 us; the launch traced here: 49 us
  Pallas kernels  45.7 us (93%)
  local copies, waits for them, and re-layouts  2.62 us (5%)
  between operations  0.64 us (1%)
    pallas_call x1, Pallas kernels, shards(): pl.pallas_call(functools.partial(layer_kernel, tp_count), out_shape=(jax....  45.7 us
    unnamed x2, local copies, waits for them, and re-layouts  2.62 us

profile of v1, /device:TPU:136, one launch (start us, length us, event | category | flops | bytes accessed | tf_op | source)
XLA Modules:
  0.0 49.0 jit_solution(9620582057817055221)
XLA Ops:
  0.6 45.7 %layer.1 = (bf16[32,384]{1,0:T(8,128)(2,1)}, f32[6,32]{1,0:T(8,128)}) custom-call(bf16[32,384]{1,0:T(8,128)(2,1)} %q_ref.1, bf16[32,384]{1,0:T(8,128)(2,1)} %new_keys.1, bf16[32,384]{1,0:T(8,128)(2,1)} %new_values.1, f32[6,32]{1,0:T(8,128)} %logit_ref.1, bf16[2048,384]{1,0:T(8,128)(2,1)} %cache_keys.1, bf16[2048,384]{1,0:T(8,128)(2,1)} %cache_values.1, ...), custom_call_target="tpu_custom_call" | custom-call | tf_op jit(solution)/shard_map/layer/pallas_call | solution.py:390
  46.4 1.3 %copy.15 = bf16[32,384]{1,0:T(8,128)(2,1)} copy(bf16[32,384]{1,0:T(8,128)(2,1)} %get-tuple-element.4) | data formatting | bytes 49152
  47.7 1.3 %copy.16 = f32[6,32]{1,0:T(8,128)} copy(f32[6,32]{1,0:T(8,128)} %get-tuple-element.5) | data formatting | bytes 1536

commit v2 on v1

v2 whole, which is shorter than its diff:
```python
import functools

import jax
import jax.numpy as jnp
from jax import lax
from jax.experimental import pallas as pl
from jax.experimental.pallas import tpu as pltpu
from jax.sharding import PartitionSpec as P

HEAD_DIM = 64
PAGE = 128
CHIPS = 8
GROUP = 16
DEAD = 1e30
MESH = pl.DeviceIdType.MESH


def thirds(x):
    high = x.astype(jnp.bfloat16)
    rest = x - high.astype(jnp.float32)
    middle = rest.astype(jnp.bfloat16)
    low = (rest - middle.astype(jnp.float32)).astype(jnp.bfloat16)
    return high, middle, low


def merge_weights(logs, spread, heads):
    top = functools.reduce(jnp.maximum, logs)
    shares = [jnp.exp(log - top) for log in logs]
    whole = functools.reduce(jnp.add, shares)
    stacked = jnp.concatenate([share / whole for share in shares], axis=0)
    lane = lax.broadcasted_iota(jnp.int32, stacked.shape, 1)
    stacked = jnp.where(lane < heads, stacked, 0.0)
    high, middle, _ = thirds(stacked)
    factors = jnp.dot(
        jnp.concatenate([high, middle], axis=1), spread, preferred_element_type=jnp.float32
    )
    return factors, top + jnp.log(whole)


def read_logs(stat):
    stat = stat.astype(jnp.float32)
    return stat + pltpu.roll(stat, PAGE - 8, 1) + pltpu.roll(stat, PAGE - 16, 1)


def write_logs(logs, heads):
    lane = lax.broadcasted_iota(jnp.int32, logs.shape, 1)
    high, middle, low = (
        part.astype(jnp.float32) for part in thirds(jnp.where(lane < heads, logs, 0.0))
    )
    packed = high + pltpu.roll(middle, 8, 1) + pltpu.roll(low, 16, 1)
    return packed.astype(jnp.bfloat16)


def layer_kernel(
    tp_count,
    q_ref,
    new_keys,
    new_values,
    logit_in,
    cache_keys,
    cache_values,
    decay_in,
    page_ref,
    length_ref,
    residual_in,
    out_weight,
    out_ref,
    forget_ref,
    keys,
    values,
    weight,
    logit_ref,
    decay_ref,
    residual_ref,
    costs,
    queries,
    forget_tile,
    forget_all,
    spread,
    parts_out,
    pair_in,
    merged,
    parts_in,
    shares_out,
    shares_in,
    local_sem,
    query_send,
    query_recv,
    forget_send,
    forget_recv,
    pair_send,
    pair_recv,
    part_send,
    part_recv,
    share_send,
    share_recv,
):
    rows, width = q_ref.shape
    heads = width // HEAD_DIM
    pairs = heads // 2
    slots = cache_keys.shape[0]
    all_keys = keys.shape[0]
    seq = lax.axis_index("seq")
    tp = lax.axis_index("tp")
    request = seq // GROUP
    chip = (seq % GROUP) // 2
    core = seq % 2

    def device(chip_step, other):
        there = (chip + chip_step) % CHIPS
        return (request * GROUP + there * 2 + (1 - core if other else core), tp)

    barrier = pltpu.get_barrier_semaphore()
    peers = [(step, other) for step in range(CHIPS) for other in (0, 1) if step or other]
    for step, other in peers:
        pl.semaphore_signal(barrier, inc=1, device_id=device(step, other), device_id_type=MESH)
    for step in range(1, tp_count):
        pl.semaphore_signal(
            barrier, inc=1, device_id=(seq, (tp + step) % tp_count), device_id_type=MESH
        )

    local = [
        pltpu.make_async_copy(source, target, local_sem.at[i])
        for i, (source, target) in enumerate(
            [
                (logit_in, logit_ref),
                (q_ref, queries.at[0, 0]),
                (decay_in, decay_ref),
                (new_keys, keys.at[pl.ds(slots, rows)]),
                (new_values, values.at[pl.ds(slots, rows)]),
                (cache_keys, keys.at[pl.ds(0, slots)]),
                (cache_values, values.at[pl.ds(0, slots)]),
                (out_weight, weight),
                (residual_in, residual_ref),
            ]
        )
    ]
    for copy in local:
        copy.start()

    pad = all_keys - slots - rows
    keys[pl.ds(slots + rows, pad), :] = jnp.zeros((pad, width), keys.dtype)
    values[pl.ds(slots + rows, pad), :] = jnp.zeros((pad, width), values.dtype)
    forget_tile[...] = jnp.zeros(forget_tile.shape, jnp.float32)
    spread_row = lax.broadcasted_iota(jnp.int32, spread.shape, 0) % PAGE
    spread_lane = lax.broadcasted_iota(jnp.int32, spread.shape, 1) // HEAD_DIM
    spread[...] = jnp.where(spread_row == spread_lane, 1.0, 0.0).astype(spread.dtype)
    local[0].wait()
    logit = logit_ref[...]
    forget_tile[pl.ds(0, heads), pl.ds(0, rows)] = -jnp.log1p(jnp.exp(-logit))
    lane = lax.broadcasted_iota(jnp.int32, forget_tile.shape, 1)
    running = forget_tile[...]
    reach = 1
    while reach < rows:
        running = running + jnp.where(lane >= reach, pltpu.roll(running, reach, 1), 0.0)
        reach *= 2
    total = jnp.sum(jnp.where(lane == rows - 1, running, 0.0), axis=1, keepdims=True)
    forget_tile[...] = jnp.broadcast_to(total, forget_tile.shape)
    pl.semaphore_wait(barrier, len(peers) + tp_count - 1)

    def query_direct(step, other):
        back = (CHIPS - step) % CHIPS
        return pltpu.make_async_remote_copy(
            src_ref=q_ref,
            dst_ref=queries.at[back, other],
            send_sem=query_send.at[step, other],
            recv_sem=query_recv.at[back, other],
            device_id=device(step, other),
            device_id_type=MESH,
        )

    def query_relay(step):
        return pltpu.make_async_remote_copy(
            src_ref=queries.at[step, 0],
            dst_ref=queries.at[step, 1],
            send_sem=query_send.at[8 - step, 1],
            recv_sem=query_recv.at[step, 1],
            device_id=device(0, 1),
            device_id_type=MESH,
        )

    def forget_copy(step, other):
        return pltpu.make_async_remote_copy(
            src_ref=forget_tile,
            dst_ref=forget_all.at[(CHIPS - step) % CHIPS, other],
            send_sem=forget_send.at[step, other],
            recv_sem=forget_recv.at[(CHIPS - step) % CHIPS, other],
            device_id=device(step, other),
            device_id_type=MESH,
        )

    for step, other in peers:
        forget_copy(step, other).start()
    first_sends = [(0, 1), (1, 0), (1, 1)]
    later_sends = [(step, 0) for step in (4, 5, 3, 6, 7, 2)]
    for step, other in first_sends + later_sends:
        query_direct(step, other).start()

    local[2].wait()
    length = length_ref[request]
    page_lane = lax.broadcasted_iota(jnp.int32, (1, PAGE), 1)
    for page in range(slots // PAGE):
        alive = page_ref[page] * PAGE + page_lane < length
        at = pl.ds(page * PAGE, PAGE)
        costs[pl.ds(0, heads), at] = jnp.where(alive, decay_ref[:, at], DEAD)
    for i in (1, 3, 4, 5, 6, 7, 8):
        local[i].wait()

    for step, other in peers:
        forget_copy((CHIPS - step) % CHIPS, other).wait_recv()
    own_forget = running
    for step, other in peers:
        earlier = (core == 1) if step == 0 else (chip + step >= CHIPS)
        own_forget = own_forget + jnp.where(earlier, forget_all[step, other], 0.0)
    forget_ref[...] = own_forget[:heads, :rows]
    costs[:, pl.ds(slots, PAGE)] = jnp.where(lane < rows, own_forget, DEAD)
    for step, other in first_sends:
        query_direct(step, other).wait_recv()

    span = 2
    chunk = span * 2 * rows
    left = lax.broadcasted_iota(jnp.int32, (chunk, 2 * HEAD_DIM), 1) < HEAD_DIM
    key_lane = lax.broadcasted_iota(jnp.int32, (chunk, PAGE), 1)
    row_index = lax.broadcasted_iota(jnp.int32, (chunk, PAGE), 0)

    def pair_copy(step):
        return pltpu.make_async_remote_copy(
            src_ref=parts_out.at[step, 1],
            dst_ref=pair_in.at[step],
            send_sem=pair_send.at[step],
            recv_sem=pair_recv.at[step],
            device_id=device(0, 1),
            device_id_type=MESH,
        )

    def part_copy(step):
        back = (CHIPS - step) % CHIPS
        return pltpu.make_async_remote_copy(
            src_ref=merged.at[step],
            dst_ref=parts_in.at[back],
            send_sem=part_send.at[step],
            recv_sem=part_recv.at[back],
            device_id=device(step, 0),
            device_id_type=MESH,
        )

    def steps_of(index):
        first = 2 * ((index // 2 + index % 2) % 2) + index // 2
        return [first, CHIPS - 1 - first]

    def join_pair(index):
        steps = steps_of(index)
        for step in steps:
            pair_copy(step).wait_recv()
        mine = jnp.concatenate([parts_out[step, 0] for step in steps], axis=0)
        partner = jnp.concatenate([pair_in[step] for step in steps], axis=0)
        factors, logs = merge_weights(
            [read_logs(mine[:, width:]), read_logs(partner[:, width:])], spread[...], heads
        )
        half = span * rows
        both = factors[:half] * mine[:, :width].astype(jnp.float32) + factors[
            half:
        ] * partner[:, :width].astype(jnp.float32)
        both = both.astype(jnp.bfloat16)
        stat = write_logs(logs, heads)
        for i, step in enumerate(steps):
            here = slice(i * rows, (i + 1) * rows)
            merged[step, :, pl.ds(0, width)] = both[here]
            merged[step, :, pl.ds(width, PAGE)] = stat[here]
        for step in steps:

            @pl.when(step > 0)
            def _():
                part_copy(step).start()

    def attend(index, between):
        steps = steps_of(index)
        fresh = None
        for i, step in enumerate(steps):
            for other in (0, 1):
                first = (2 * i + other) * rows
                offset = row_index - first
                inside = (offset >= 0) & (offset < rows)
                later = jnp.where(
                    step == 0, jnp.where(core + other == 1, 1 - core, 0), (chip + step < CHIPS) * 1
                )
                own = jnp.where(step == 0, 1 - other, 0)
                limit = jnp.where(own == 1, offset, jnp.where(later == 1, rows, -1))
                fresh = jnp.where(inside, limit, 0 if fresh is None else fresh)
        visible = key_lane <= fresh
        packed = jnp.zeros((chunk, PAGE), jnp.float32)
        for pair in range(pairs):
            if pair == pairs - 1:
                between()
            at = slice(pair * 2 * HEAD_DIM, (pair + 1) * 2 * HEAD_DIM)
            q = jnp.concatenate(
                [queries[step, other, :, at] for step in steps for other in (0, 1)], axis=0
            )
            q = q * jnp.asarray(HEAD_DIM**-0.5, q.dtype)
            zero = jnp.zeros_like(q)
            value_pair = jnp.concatenate(
                [values[:, at], jnp.ones((all_keys, 2 * HEAD_DIM), values.dtype)], axis=1
            )
            both = []
            for side in (0, 1):
                head = pair * 2 + side
                q_side = jnp.where(left, q, zero) if side == 0 else jnp.where(left, zero, q)
                scores = lax.dot_general(
                    q_side,
                    keys[:, at],
                    (((1,), (1,)), ((), ())),
                    preferred_element_type=jnp.float32,
                )
                scores = scores - costs[pl.ds(head, 1), :]
                old = scores[:, :slots]
                new = jnp.where(visible, scores[:, slots:], -DEAD)
                highest = jnp.maximum(
                    jnp.max(old, axis=1, keepdims=True), jnp.max(new, axis=1, keepdims=True)
                )
                weights = jnp.concatenate(
                    [
                        jnp.exp(old - highest).astype(jnp.bfloat16),
                        jnp.exp(new - highest).astype(jnp.bfloat16),
                    ],
                    axis=1,
                )
                summed = jnp.dot(weights, value_pair, preferred_element_type=jnp.float32)
                sums = summed[:, 2 * HEAD_DIM :]
                both.append(summed[:, : 2 * HEAD_DIM] / sums)
                packed = jnp.where(key_lane == head, highest + jnp.log(sums), packed)
            out = jnp.where(left, both[0], both[1]).astype(jnp.bfloat16)
            for i in range(2 * span):
                parts_out[steps[i // 2], i % 2, :, at] = out[i * rows : (i + 1) * rows]
        stat = write_logs(packed, heads)
        for i in range(2 * span):
            parts_out[steps[i // 2], i % 2, :, pl.ds(width, PAGE)] = stat[
                i * rows : (i + 1) * rows
            ]
        for step in steps:
            pair_copy(step).start()

    turns = CHIPS // span

    def turn(index, _):
        @pl.when(index > 0)
        def _():
            for step in steps_of(index):
                query_relay(step).wait_recv()

        def between():
            @pl.when(index < turns - 1)
            def _():
                for step in steps_of(index + 1):
                    query_direct(CHIPS - step, 0).wait_recv()
                    query_relay(step).start()

            @pl.when(index > 0)
            def _():
                join_pair(index - 1)

        attend(index, between)
        return 0

    lax.fori_loop(0, turns, turn, 0)
    join_pair(turns - 1)

    for step in range(1, CHIPS):
        part_copy(CHIPS - step).wait_recv()

    def part(step, at):
        return parts_in[step, :, at] if step else merged[0, :, at]

    factors, _ = merge_weights(
        [read_logs(part(step, pl.ds(width, PAGE))) for step in range(CHIPS)], spread[...], heads
    )
    attention = jnp.zeros((rows, width), jnp.float32)
    for step in range(CHIPS):
        attention = attention + factors[step * rows : (step + 1) * rows] * part(
            step, pl.ds(0, width)
        ).astype(jnp.float32)
    attention = attention.astype(jnp.bfloat16)

    def share_copy(step):
        return pltpu.make_async_remote_copy(
            src_ref=shares_out.at[step - 1],
            dst_ref=shares_in.at[tp_count - step - 1],
            send_sem=share_send.at[step - 1],
            recv_sem=share_recv.at[tp_count - step - 1],
            device_id=(seq, (tp + step) % tp_count),
            device_id_type=MESH,
        )

    def share(step):
        block = (tp + step) % tp_count
        columns = pl.ds(pl.multiple_of(block * width, PAGE), width)
        return jnp.dot(attention, weight[:, columns], preferred_element_type=jnp.float32)

    for step in (2, 1, 3)[: tp_count - 1]:
        shares_out[step - 1] = share(step).astype(jnp.bfloat16)
        share_copy(step).start()
    summed = share(0) + residual_ref[...].astype(jnp.float32)
    for step in range(1, tp_count):
        share_copy(step).wait_recv()
        summed = summed + shares_in[tp_count - step - 1].astype(jnp.float32)
    out_ref[...] = summed.astype(out_ref.dtype)

    for step, other in first_sends + later_sends:
        query_direct(step, other).wait_send()
    for step in range(1, CHIPS - 1):
        query_relay(step).wait_send()
    for step, other in peers:
        forget_copy(step, other).wait_send()
    for step in range(CHIPS):
        pair_copy(step).wait_send()
        if step:
            part_copy(step).wait_send()
    for step in range(1, tp_count):
        share_copy(step).wait_send()


def shards(
    queries,
    new_keys,
    new_values,
    forget_logit,
    cache_keys,
    cache_values,
    cache_decay,
    slot_page,
    cache_len,
    residual,
    out_weight,
):
    rows, width = queries.shape
    heads = forget_logit.shape[0]
    slots = cache_keys.shape[0]
    tp_count = lax.axis_size("tp")
    vmem = pl.BlockSpec(memory_space=pltpu.VMEM)
    smem = pl.BlockSpec(memory_space=pltpu.SMEM)
    anywhere = pl.BlockSpec(memory_space=pl.ANY)
    dma = pltpu.SemaphoreType.DMA
    half = jnp.bfloat16
    single = jnp.float32
    return pl.pallas_call(
        functools.partial(layer_kernel, tp_count),
        out_shape=(
            jax.ShapeDtypeStruct((rows, width), half),
            jax.ShapeDtypeStruct((heads, rows), single),
        ),
        in_specs=[
            anywhere, anywhere, anywhere, anywhere, anywhere, anywhere, anywhere, smem, smem,
            anywhere, anywhere,
        ],
        out_specs=(vmem, vmem),
        scratch_shapes=[
            pltpu.VMEM((slots + PAGE, width), half),
            pltpu.VMEM((slots + PAGE, width), half),
            pltpu.VMEM(out_weight.shape, half),
            pltpu.VMEM(forget_logit.shape, single),
            pltpu.VMEM(cache_decay.shape, single),
            pltpu.VMEM(residual.shape, half),
            pltpu.VMEM((8, slots + PAGE), single),
            pltpu.VMEM((CHIPS, 2, rows, width), half),
            pltpu.VMEM((8, PAGE), single),
            pltpu.VMEM((CHIPS, 2, 8, PAGE), single),
            pltpu.VMEM((2 * PAGE, width), half),
            pltpu.VMEM((CHIPS, 2, rows, width + PAGE), half),
            pltpu.VMEM((CHIPS, rows, width + PAGE), half),
            pltpu.VMEM((CHIPS, rows, width + PAGE), half),
            pltpu.VMEM((CHIPS, rows, width + PAGE), half),
            pltpu.VMEM((max(tp_count - 1, 1), rows, width), half),
            pltpu.VMEM((max(tp_count - 1, 1), rows, width), half),
            dma((9,)),
            dma((CHIPS, 2)),
            dma((CHIPS, 2)),
            dma((CHIPS, 2)),
            dma((CHIPS, 2)),
            dma((CHIPS,)),
            dma((CHIPS,)),
            dma((CHIPS,)),
            dma((CHIPS,)),
            dma((max(tp_count - 1, 1),)),
            dma((max(tp_count - 1, 1),)),
        ],
        compiler_params=pltpu.CompilerParams(
            collective_id=0, has_side_effects=True, vmem_limit_bytes=60 * 1024 * 1024
        ),
        name="layer",
    )(
        queries, new_keys, new_values, forget_logit, cache_keys, cache_values, cache_decay,
        slot_page, cache_len, residual, out_weight,
    )


def solution(mesh):
    return jax.shard_map(
        shards,
        mesh=mesh,
        in_specs=(
            P("seq", "tp"),
            P("seq", "tp"),
            P("seq", "tp"),
            P("tp", "seq"),
            P("seq", "tp"),
            P("seq", "tp"),
            P("tp", "seq"),
            P("seq"),
            P(),
            P("seq", "tp"),
            P("tp", None),
        ),
        out_specs=(P("seq", "tp"), P("tp", "seq")),
        check_vma=False,
    )
```

time: 49.2 us -> 44.5 us (0.904)
  the two profiles are of different devices: /device:TPU:136 before, /device:TPU:1 now
where the time goes in v2:
time: 44.5 us; the launch traced here: 44.3 us
  Pallas kernels  41 us (92%)
  local copies, waits for them, and re-layouts  2.62 us (6%)
  between operations  0.64 us (1%)
    pallas_call x1, Pallas kernels, shards(): pl.pallas_call(functools.partial(layer_kernel, tp_count), out_shape=(jax....  41 us
    unnamed x2, local copies, waits for them, and re-layouts  2.62 us

profile of v2, /device:TPU:1, one launch (start us, length us, event | category | flops | bytes accessed | tf_op | source)
XLA Modules:
  0.0 44.3 jit_solution(1742230930915153622)
XLA Ops:
  0.6 41.0 %layer.1 = (bf16[32,384]{1,0:T(8,128)(2,1)}, f32[6,32]{1,0:T(8,128)}) custom-call(bf16[32,384]{1,0:T(8,128)(2,1)} %q_ref.1, bf16[32,384]{1,0:T(8,128)(2,1)} %new_keys.1, bf16[32,384]{1,0:T(8,128)(2,1)} %new_values.1, f32[6,32]{1,0:T(8,128)} %logit_in.1, bf16[2048,384]{1,0:T(8,128)(2,1)} %cache_keys.1, bf16[2048,384]{1,0:T(8,128)(2,1)} %cache_values.1, ...), custom_call_target="tpu_custom_call" | custom-call | tf_op jit(solution)/shard_map/layer/pallas_call | solution.py:444
  41.6 1.3 %copy.15 = bf16[32,384]{1,0:T(8,128)(2,1)} copy(bf16[32,384]{1,0:T(8,128)(2,1)} %get-tuple-element.4) | data formatting | bytes 49152
  43.0 1.3 %copy.16 = f32[6,32]{1,0:T(8,128)} copy(f32[6,32]{1,0:T(8,128)} %get-tuple-element.5) | data formatting | bytes 1536

commit v3 on v2

--- a/solution.py
+++ b/solution.py
@@ -12,6 +12,7 @@
 CHIPS = 8
 GROUP = 16
 DEAD = 1e30
+BETWEEN = 4
 MESH = pl.DeviceIdType.MESH
 
 
@@ -75,6 +76,7 @@
     costs,
     queries,
     forget_tile,
+    forget_row,
     forget_all,
     spread,
     parts_out,
@@ -155,7 +157,8 @@
         running = running + jnp.where(lane >= reach, pltpu.roll(running, reach, 1), 0.0)
         reach *= 2
     total = jnp.sum(jnp.where(lane == rows - 1, running, 0.0), axis=1, keepdims=True)
-    forget_tile[...] = jnp.broadcast_to(total, forget_tile.shape)
+    head_row = lax.broadcasted_iota(jnp.int32, forget_tile.shape, 0)
+    forget_row[...] = jnp.sum(jnp.where(head_row == lane, total, 0.0), axis=0, keepdims=True)
     pl.semaphore_wait(barrier, len(peers) + tp_count - 1)
 
     def query_direct(step, other):
@@ -181,7 +184,7 @@
 
     def forget_copy(step, other):
         return pltpu.make_async_remote_copy(
-            src_ref=forget_tile,
+            src_ref=forget_row,
             dst_ref=forget_all.at[(CHIPS - step) % CHIPS, other],
             send_sem=forget_send.at[step, other],
             recv_sem=forget_recv.at[(CHIPS - step) % CHIPS, other],
@@ -191,8 +194,8 @@
 
     for step, other in peers:
         forget_copy(step, other).start()
-    first_sends = [(0, 1), (1, 0), (1, 1)]
-    later_sends = [(step, 0) for step in (4, 5, 3, 6, 7, 2)]
+    first_sends = [(0, 1), (6, 0), (6, 1)]
+    later_sends = [(step, 0) for step in (4, 3, 5, 2, 7, 1)]
     for step, other in first_sends + later_sends:
         query_direct(step, other).start()
 
@@ -208,10 +211,13 @@
 
     for step, other in peers:
         forget_copy((CHIPS - step) % CHIPS, other).wait_recv()
-    own_forget = running
+    before = jnp.zeros(forget_row.shape, jnp.float32)
     for step, other in peers:
         earlier = (core == 1) if step == 0 else (chip + step >= CHIPS)
-        own_forget = own_forget + jnp.where(earlier, forget_all[step, other], 0.0)
+        before = before + jnp.where(earlier, forget_all[step, other], 0.0)
+    own_forget = running + jnp.sum(
+        jnp.where(head_row == lane, before, 0.0), axis=1, keepdims=True
+    )
     forget_ref[...] = own_forget[:heads, :rows]
     costs[:, pl.ds(slots, PAGE)] = jnp.where(lane < rows, own_forget, DEAD)
     for step, other in first_sends:
@@ -245,8 +251,8 @@
         )
 
     def steps_of(index):
-        first = 2 * ((index // 2 + index % 2) % 2) + index // 2
-        return [first, CHIPS - 1 - first]
+        later = (index + 3) // 4
+        return [later * (4 - index * (index - 1) // 2), 2 + later * (2 + index)]
 
     def join_pair(index):
         steps = steps_of(index)
@@ -289,45 +295,59 @@
                 fresh = jnp.where(inside, limit, 0 if fresh is None else fresh)
         visible = key_lane <= fresh
         packed = jnp.zeros((chunk, PAGE), jnp.float32)
-        for pair in range(pairs):
-            if pair == pairs - 1:
-                between()
-            at = slice(pair * 2 * HEAD_DIM, (pair + 1) * 2 * HEAD_DIM)
+
+        def columns(pair):
+            return slice(pair * 2 * HEAD_DIM, (pair + 1) * 2 * HEAD_DIM)
+
+        def scores_of(head):
+            at = columns(head // 2)
             q = jnp.concatenate(
                 [queries[step, other, :, at] for step in steps for other in (0, 1)], axis=0
             )
             q = q * jnp.asarray(HEAD_DIM**-0.5, q.dtype)
             zero = jnp.zeros_like(q)
+            q = jnp.where(left, zero, q) if head % 2 else jnp.where(left, q, zero)
+            return lax.dot_general(
+                q, keys[:, at], (((1,), (1,)), ((), ())), preferred_element_type=jnp.float32
+            )
+
+        def weigh(head, scores):
+            cost = costs[pl.ds(head, 1), :]
+            old = scores[:, :slots] - cost[:, :slots]
+            new = jnp.where(visible, scores[:, slots:] - cost[:, slots:], -DEAD)
+            highest = jnp.maximum(
+                jnp.max(old, axis=1, keepdims=True), jnp.max(new, axis=1, keepdims=True)
+            )
+            weights = jnp.concatenate(
+                [
+                    jnp.exp(old - highest).astype(jnp.bfloat16),
+                    jnp.exp(new - highest).astype(jnp.bfloat16),
+                ],
+                axis=1,
+            )
             value_pair = jnp.concatenate(
-                [values[:, at], jnp.ones((all_keys, 2 * HEAD_DIM), values.dtype)], axis=1
+                [
+                    values[:, columns(head // 2)],
+                    jnp.ones((all_keys, 2 * HEAD_DIM), values.dtype),
+                ],
+                axis=1,
             )
+            summed = jnp.dot(weights, value_pair, preferred_element_type=jnp.float32)
+            sums = summed[:, 2 * HEAD_DIM :]
+            return summed[:, : 2 * HEAD_DIM] / sums, highest + jnp.log(sums)
+
+        ahead = scores_of(0)
+        for pair in range(pairs):
+            at = columns(pair)
             both = []
-            for side in (0, 1):
-                head = pair * 2 + side
-                q_side = jnp.where(left, q, zero) if side == 0 else jnp.where(left, zero, q)
-                scores = lax.dot_general(
-                    q_side,
-                    keys[:, at],
-                    (((1,), (1,)), ((), ())),
-                    preferred_element_type=jnp.float32,
-                )
-                scores = scores - costs[pl.ds(head, 1), :]
-                old = scores[:, :slots]
-                new = jnp.where(visible, scores[:, slots:], -DEAD)
-                highest = jnp.maximum(
-                    jnp.max(old, axis=1, keepdims=True), jnp.max(new, axis=1, keepdims=True)
-                )
-                weights = jnp.concatenate(
-                    [
-                        jnp.exp(old - highest).astype(jnp.bfloat16),
-                        jnp.exp(new - highest).astype(jnp.bfloat16),
-                    ],
-                    axis=1,
-                )
-                summed = jnp.dot(weights, value_pair, preferred_element_type=jnp.float32)
-                sums = summed[:, 2 * HEAD_DIM :]
-                both.append(summed[:, : 2 * HEAD_DIM] / sums)
-                packed = jnp.where(key_lane == head, highest + jnp.log(sums), packed)
+            for head in (2 * pair, 2 * pair + 1):
+                if head == BETWEEN:
+                    between()
+                scores = ahead
+                ahead = scores_of(head + 1) if head + 1 < heads else None
+                mean, log = weigh(head, scores)
+                both.append(mean)
+                packed = jnp.where(key_lane == head, log, packed)
             out = jnp.where(left, both[0], both[1]).astype(jnp.bfloat16)
             for i in range(2 * span):
                 parts_out[steps[i // 2], i % 2, :, at] = out[i * rows : (i + 1) * rows]
@@ -406,7 +426,7 @@
 
     for step, other in first_sends + later_sends:
         query_direct(step, other).wait_send()
-    for step in range(1, CHIPS - 1):
+    for step in (1, 3, 4, 5, 6, 7):
         query_relay(step).wait_send()
     for step, other in peers:
         forget_copy(step, other).wait_send()
@@ -462,7 +482,8 @@
             pltpu.VMEM((8, slots + PAGE), single),
             pltpu.VMEM((CHIPS, 2, rows, width), half),
             pltpu.VMEM((8, PAGE), single),
-            pltpu.VMEM((CHIPS, 2, 8, PAGE), single),
+            pltpu.VMEM((1, PAGE), single),
+            pltpu.VMEM((CHIPS, 2, 1, PAGE), single),
             pltpu.VMEM((2 * PAGE, width), half),
             pltpu.VMEM((CHIPS, 2, rows, width + PAGE), half),
             pltpu.VMEM((CHIPS, rows, width + PAGE), half),

time: 44.5 us -> 41.3 us (0.928)
  Pallas kernels: 41 us -> 37.8 us
    pallas_call x1, Pallas kernels: 41 us -> 37.8 us  [shards(): pl.pallas_call(functools.partial(layer_kernel, tp_count), out_shape=(jax....]
where the time goes in v3:
time: 41.3 us; the launch traced here: 41 us
  Pallas kernels  37.8 us (92%)
  local copies, waits for them, and re-layouts  2.62 us (6%)
  between operations  0.64 us (2%)
    pallas_call x1, Pallas kernels, shards(): pl.pallas_call(functools.partial(layer_kernel, tp_count), out_shape=(jax....  37.8 us
    unnamed x2, local copies, waits for them, and re-layouts  2.62 us

profile of v3, /device:TPU:1, one launch (start us, length us, event | category | flops | bytes accessed | tf_op | source)
XLA Modules:
  0.0 41.0 jit_solution(11432923958162837085)
XLA Ops:
  0.6 37.8 %layer.1 = (bf16[32,384]{1,0:T(8,128)(2,1)}, f32[6,32]{1,0:T(8,128)}) custom-call(bf16[32,384]{1,0:T(8,128)(2,1)} %q_ref.1, bf16[32,384]{1,0:T(8,128)(2,1)} %new_keys.1, bf16[32,384]{1,0:T(8,128)(2,1)} %new_values.1, f32[6,32]{1,0:T(8,128)} %logit_in.1, bf16[2048,384]{1,0:T(8,128)(2,1)} %cache_keys.1, bf16[2048,384]{1,0:T(8,128)(2,1)} %cache_values.1, ...), custom_call_target="tpu_custom_call" | custom-call | tf_op jit(solution)/shard_map/layer/pallas_call | solution.py:464
  38.4 1.3 %copy.15 = bf16[32,384]{1,0:T(8,128)(2,1)} copy(bf16[32,384]{1,0:T(8,128)(2,1)} %get-tuple-element.4) | data formatting | bytes 49152
  39.7 1.3 %copy.16 = f32[6,32]{1,0:T(8,128)} copy(f32[6,32]{1,0:T(8,128)} %get-tuple-element.5) | data formatting | bytes 1536

commit v4 on v3

--- a/solution.py
+++ b/solution.py
@@ -12,7 +12,7 @@
 CHIPS = 8
 GROUP = 16
 DEAD = 1e30
-BETWEEN = 4
+BETWEEN = 3
 MESH = pl.DeviceIdType.MESH
 
 
@@ -83,6 +83,7 @@
     pair_in,
     merged,
     parts_in,
+    last_in,
     shares_out,
     shares_in,
     local_sem,
@@ -94,6 +95,8 @@
     pair_recv,
     part_send,
     part_recv,
+    last_send,
+    last_recv,
     share_send,
     share_recv,
 ):
@@ -249,6 +252,19 @@
             device_id=device(step, 0),
             device_id_type=MESH,
         )
+
+    def last_copy(step, other):
+        back = CHIPS - step
+        return pltpu.make_async_remote_copy(
+            src_ref=parts_out.at[step, other],
+            dst_ref=last_in.at[back // (CHIPS - 1), other],
+            send_sem=last_send.at[step // (CHIPS - 1), other],
+            recv_sem=last_recv.at[back // (CHIPS - 1), other],
+            device_id=device(step, other),
+            device_id_type=MESH,
+        )
+
+    last_blocks = [(step, other) for step in (1, CHIPS - 1) for other in (0, 1)]
 
     def steps_of(index):
         later = (index + 3) // 4
@@ -356,8 +372,11 @@
             parts_out[steps[i // 2], i % 2, :, pl.ds(width, PAGE)] = stat[
                 i * rows : (i + 1) * rows
             ]
-        for step in steps:
-            pair_copy(step).start()
+
+        @pl.when(index < turns - 1)
+        def _():
+            for step in steps:
+                pair_copy(step).start()
 
     turns = CHIPS // span
 
@@ -382,22 +401,24 @@
         return 0
 
     lax.fori_loop(0, turns, turn, 0)
-    join_pair(turns - 1)
-
-    for step in range(1, CHIPS):
+    for step, other in last_blocks:
+        last_copy(step, other).start()
+
+    middle_steps = range(2, CHIPS - 1)
+    for step in middle_steps:
         part_copy(CHIPS - step).wait_recv()
-
-    def part(step, at):
-        return parts_in[step, :, at] if step else merged[0, :, at]
-
+    for step, other in last_blocks:
+        last_copy(CHIPS - step, other).wait_recv()
+    parts = [merged.at[0]] + [parts_in.at[step] for step in middle_steps]
+    parts += [last_in.at[side, other] for side in (0, 1) for other in (0, 1)]
     factors, _ = merge_weights(
-        [read_logs(part(step, pl.ds(width, PAGE))) for step in range(CHIPS)], spread[...], heads
+        [read_logs(part[:, pl.ds(width, PAGE)]) for part in parts], spread[...], heads
     )
     attention = jnp.zeros((rows, width), jnp.float32)
-    for step in range(CHIPS):
-        attention = attention + factors[step * rows : (step + 1) * rows] * part(
-            step, pl.ds(0, width)
-        ).astype(jnp.float32)
+    for i, part in enumerate(parts):
+        attention = attention + factors[i * rows : (i + 1) * rows] * part[
+            :, pl.ds(0, width)
+        ].astype(jnp.float32)
     attention = attention.astype(jnp.bfloat16)
 
     def share_copy(step):
@@ -430,10 +451,12 @@
         query_relay(step).wait_send()
     for step, other in peers:
         forget_copy(step, other).wait_send()
-    for step in range(CHIPS):
+    pair_copy(0).wait_send()
+    for step in middle_steps:
         pair_copy(step).wait_send()
-        if step:
-            part_copy(step).wait_send()
+        part_copy(step).wait_send()
+    for step, other in last_blocks:
+        last_copy(step, other).wait_send()
     for step in range(1, tp_count):
         share_copy(step).wait_send()
 
@@ -489,6 +512,7 @@
             pltpu.VMEM((CHIPS, rows, width + PAGE), half),
             pltpu.VMEM((CHIPS, rows, width + PAGE), half),
             pltpu.VMEM((CHIPS, rows, width + PAGE), half),
+            pltpu.VMEM((2, 2, rows, width + PAGE), half),
             pltpu.VMEM((max(tp_count - 1, 1), rows, width), half),
             pltpu.VMEM((max(tp_count - 1, 1), rows, width), half),
             dma((9,)),
@@ -500,6 +524,8 @@
             dma((CHIPS,)),
             dma((CHIPS,)),
             dma((CHIPS,)),
+            dma((2, 2)),
+            dma((2, 2)),
             dma((max(tp_count - 1, 1),)),
             dma((max(tp_count - 1, 1),)),
         ],

time: 41.3 us -> 41.8 us (1.012)
  Pallas kernels: 37.8 us -> 38.3 us
    pallas_call x1, Pallas kernels: 37.8 us -> 38.3 us  [shards(): pl.pallas_call(functools.partial(layer_kernel, tp_count), out_shape=(jax....]
where the time goes in v4:
time: 41.8 us; the launch traced here: 41.5 us
  Pallas kernels  38.3 us (92%)
  local copies, waits for them, and re-layouts  2.62 us (6%)
  between operations  0.64 us (2%)
    pallas_call x1, Pallas kernels, shards(): pl.pallas_call(functools.partial(layer_kernel, tp_count), out_shape=(jax....  38.3 us
    unnamed x2, local copies, waits for them, and re-layouts  2.62 us

profile of v4, /device:TPU:1, one launch (start us, length us, event | category | flops | bytes accessed | tf_op | source)
XLA Modules:
  0.0 41.5 jit_solution(8091652214310951888)
XLA Ops:
  0.6 38.3 %layer.1 = (bf16[32,384]{1,0:T(8,128)(2,1)}, f32[6,32]{1,0:T(8,128)}) custom-call(bf16[32,384]{1,0:T(8,128)(2,1)} %q_ref.1, bf16[32,384]{1,0:T(8,128)(2,1)} %new_keys.1, bf16[32,384]{1,0:T(8,128)(2,1)} %new_values.1, f32[6,32]{1,0:T(8,128)} %logit_in.1, bf16[2048,384]{1,0:T(8,128)(2,1)} %cache_keys.1, bf16[2048,384]{1,0:T(8,128)(2,1)} %cache_values.1, ...), custom_call_target="tpu_custom_call" | custom-call | tf_op jit(solution)/shard_map/layer/pallas_call | solution.py:487
  38.9 1.3 %copy.15 = bf16[32,384]{1,0:T(8,128)(2,1)} copy(bf16[32,384]{1,0:T(8,128)(2,1)} %get-tuple-element.4) | data formatting | bytes 49152
  40.3 1.3 %copy.16 = f32[6,32]{1,0:T(8,128)} copy(f32[6,32]{1,0:T(8,128)} %get-tuple-element.5) | data formatting | bytes 1536

commit v5 on v3

--- a/solution.py
+++ b/solution.py
@@ -299,14 +299,16 @@
         def columns(pair):
             return slice(pair * 2 * HEAD_DIM, (pair + 1) * 2 * HEAD_DIM)
 
-        def scores_of(head):
-            at = columns(head // 2)
+        def scores_of(pair):
+            at = columns(pair)
             q = jnp.concatenate(
                 [queries[step, other, :, at] for step in steps for other in (0, 1)], axis=0
             )
             q = q * jnp.asarray(HEAD_DIM**-0.5, q.dtype)
             zero = jnp.zeros_like(q)
-            q = jnp.where(left, zero, q) if head % 2 else jnp.where(left, q, zero)
+            q = jnp.concatenate(
+                [jnp.where(left, q, zero), jnp.where(left, zero, q)], axis=0
+            )
             return lax.dot_general(
                 q, keys[:, at], (((1,), (1,)), ((), ())), preferred_element_type=jnp.float32
             )
@@ -343,8 +345,11 @@
             for head in (2 * pair, 2 * pair + 1):
                 if head == BETWEEN:
                     between()
-                scores = ahead
-                ahead = scores_of(head + 1) if head + 1 < heads else None
+                if head % 2 == 0:
+                    pair_scores = ahead
+                    ahead = scores_of(pair + 1) if pair + 1 < pairs else None
+                first = head % 2 * chunk
+                scores = pair_scores[first : first + chunk]
                 mean, log = weigh(head, scores)
                 both.append(mean)
                 packed = jnp.where(key_lane == head, log, packed)

time: 41.3 us -> 40.3 us (0.976)
  the two profiles are of different devices: /device:TPU:1 before, /device:TPU:14 now
where the time goes in v5:
time: 40.3 us; the launch traced here: 40.1 us
  Pallas kernels  36.8 us (91%)
  local copies, waits for them, and re-layouts  2.62 us (7%)
  between operations  0.64 us (2%)
    pallas_call x1, Pallas kernels, shards(): pl.pallas_call(functools.partial(layer_kernel, tp_count), out_shape=(jax....  36.8 us
    unnamed x2, local copies, waits for them, and re-layouts  2.62 us

profile of v5, /device:TPU:14, one launch (start us, length us, event | category | flops | bytes accessed | tf_op | source)
XLA Modules:
  0.0 40.1 jit_solution(15807912258414159011)
XLA Ops:
  0.6 36.8 %layer.1 = (bf16[32,384]{1,0:T(8,128)(2,1)}, f32[6,32]{1,0:T(8,128)}) custom-call(bf16[32,384]{1,0:T(8,128)(2,1)} %q_ref.1, bf16[32,384]{1,0:T(8,128)(2,1)} %new_keys.1, bf16[32,384]{1,0:T(8,128)(2,1)} %new_values.1, f32[6,32]{1,0:T(8,128)} %logit_in.1, bf16[2048,384]{1,0:T(8,128)(2,1)} %cache_keys.1, bf16[2048,384]{1,0:T(8,128)(2,1)} %cache_values.1, ...), custom_call_target="tpu_custom_call" | custom-call | tf_op jit(solution)/shard_map/layer/pallas_call | solution.py:469
  37.5 1.3 %copy.15 = bf16[32,384]{1,0:T(8,128)(2,1)} copy(bf16[32,384]{1,0:T(8,128)(2,1)} %get-tuple-element.4) | data formatting | bytes 49152
  38.8 1.3 %copy.16 = f32[6,32]{1,0:T(8,128)} copy(f32[6,32]{1,0:T(8,128)} %get-tuple-element.5) | data formatting | bytes 1536

commit v6 on v5

--- a/solution.py
+++ b/solution.py
@@ -12,7 +12,7 @@
 CHIPS = 8
 GROUP = 16
 DEAD = 1e30
-BETWEEN = 4
+BETWEEN = 2
 MESH = pl.DeviceIdType.MESH
 
 

time: 40.3 us -> 40.7 us (level)
  the two profiles are of different devices: /device:TPU:14 before, /device:TPU:1 now
where the time goes in v6:
time: 40.7 us; the launch traced here: 40.4 us
  Pallas kernels  37.2 us (91%)
  local copies, waits for them, and re-layouts  2.62 us (6%)
  between operations  0.64 us (2%)
    pallas_call x1, Pallas kernels, shards(): pl.pallas_call(functools.partial(layer_kernel, tp_count), out_shape=(jax....  37.2 us
    unnamed x2, local copies, waits for them, and re-layouts  2.62 us

profile of v6, /device:TPU:1, one launch (start us, length us, event | category | flops | bytes accessed | tf_op | source)
XLA Modules:
  0.0 40.4 jit_solution(1923581434157146494)
XLA Ops:
  0.6 37.2 %layer.1 = (bf16[32,384]{1,0:T(8,128)(2,1)}, f32[6,32]{1,0:T(8,128)}) custom-call(bf16[32,384]{1,0:T(8,128)(2,1)} %q_ref.1, bf16[32,384]{1,0:T(8,128)(2,1)} %new_keys.1, bf16[32,384]{1,0:T(8,128)(2,1)} %new_values.1, f32[6,32]{1,0:T(8,128)} %logit_in.1, bf16[2048,384]{1,0:T(8,128)(2,1)} %cache_keys.1, bf16[2048,384]{1,0:T(8,128)(2,1)} %cache_values.1, ...), custom_call_target="tpu_custom_call" | custom-call | tf_op jit(solution)/shard_map/layer/pallas_call | solution.py:469
  37.8 1.3 %copy.15 = bf16[32,384]{1,0:T(8,128)(2,1)} copy(bf16[32,384]{1,0:T(8,128)(2,1)} %get-tuple-element.4) | data formatting | bytes 49152
  39.2 1.3 %copy.16 = f32[6,32]{1,0:T(8,128)} copy(f32[6,32]{1,0:T(8,128)} %get-tuple-element.5) | data formatting | bytes 1536
